TPU v7x, 32 devices: a whole 2x2x4 slice. The times are simulated.
32 devices in a mesh: rows: 16 (over z, y, x), genes: 2 (over core).
Axes of the slice: x: 2, y: 2, z: 4, core: 2. Of those that a mesh axis runs over, the one named last changes fastest.
Arguments:
- tokens: bfloat16 [16, 2048, 768], P('rows', 'genes'), may hold values from -6 to 6
- segment_ids: int32 [16, 2048], P('rows'), may hold values from 0 to 7, never falling along the last dimension, each value on 1 to 512 neighbouring positions
- cotangent: bfloat16 [16, 2048, 768], P('rows', 'genes'), may hold values from -6 to 6
- matrices: float32 [3, 768, 3072], P(None, ('rows', 'genes')), may hold values from -0.57735027 to 0.57735027
- vectors: float32 [12, 768], P(None, ('rows', 'genes')), may hold values from -1.2 to 1.8
- mat_first: float32 [3, 768, 3072], P(None, ('rows', 'genes')), may hold values from -135.7645 to 135.7645
- mat_second: float32 [3, 768, 3072], P(None, ('rows', 'genes')), may hold values from 327.68 to 32768
- vec_first: float32 [12, 768], P(None, ('rows', 'genes')), may hold values from -135.7645 to 135.7645
- vec_second: float32 [12, 768], P(None, ('rows', 'genes')), may hold values from 8192 to 32768
Outputs:
- layer_out: bfloat16 [16, 2048, 768], P('rows', 'genes')
- tokens_grad: float32 [16, 2048, 768], P('rows', 'genes')
- matrices_new: float32 [3, 768, 3072], P(None, ('rows', 'genes'))
- matrices_first: float32 [3, 768, 3072], P(None, ('rows', 'genes'))
- matrices_second: float32 [3, 768, 3072], P(None, ('rows', 'genes'))
- vectors_new: float32 [12, 768], P(None, ('rows', 'genes'))
- vectors_first: float32 [12, 768], P(None, ('rows', 'genes'))
- vectors_second: float32 [12, 768], P(None, ('rows', 'genes'))
Inputs may be any that keep to these rules, and one draw needn't show every extreme that they name: `segment_ids`: within a row the ids never fall; each cell holds 1 to 512 genes, one cell of each row exactly 512.
All inputs are finite; a program needn't handle non-finite values.
Results may differ from a plain program's by a relative error of at most 0.011.
Values may be sent and summed in bfloat16 or wider, within the bound.
No kernel may reach another device: no remote copies, remote signals or barrier semaphores. Data moves between devices by JAX's collectives and lax.ppermute only.
A program may use at most 256 MiB of HBM per device.

v0:
```python
import jax
import jax.numpy as jnp
from jax import lax
from jax.sharding import PartitionSpec as P

HD = 64
STEP = 10


BETA_FIRST = 0.5
BETA_SECOND = 0.5
ADAM_EPS = 1e-08
MATRIX_RATE = 0.05
VECTOR_RATE = 0.3
MATRIX_DECAY = 0.01
NORM_EPS = 1e-05
SCORE_MASK = -1e30


def norm_rows(values, gain_row, shift_row):
    centre = values - jnp.mean(values, axis=-1, keepdims=True)
    spread = jnp.mean(centre * centre, axis=-1, keepdims=True)
    return centre * lax.rsqrt(spread + NORM_EPS) * gain_row + shift_row


def gelu_exact(values):
    return jax.nn.gelu(values, approximate=False)


def contract_rows(former, latter):
    return lax.dot_general(
        former, latter, (((0,), (0,)), ((), ())), preferred_element_type=jnp.float32
    )


def contract_cols(former, latter):
    return lax.dot_general(
        former, latter, (((1,), (1,)), ((), ())), preferred_element_type=jnp.float32
    )


def masked_scores(query_block, segment_block, key_rows, segments):
    scores = jnp.einsum(
        "qhd,khd->hqk", query_block, key_rows, preferred_element_type=jnp.float32
    ) * HD ** (-0.5)
    allowed = (segment_block[:, None] == segments[None, :])[None]
    return (jnp.where(allowed, scores, SCORE_MASK), allowed)


def forward_block(query_block, segment_block, key_rows, value_rows, segments):
    scores, allowed = masked_scores(query_block, segment_block, key_rows, segments)
    largest = jnp.max(scores, axis=-1, keepdims=True)
    weights = jnp.exp(scores - largest)
    totals = jnp.sum(weights, axis=-1, keepdims=True)
    probs_low = (weights / totals).astype(jnp.bfloat16)
    context = jnp.einsum("hqk,khd->qhd", probs_low, value_rows, preferred_element_type=jnp.float32)
    return (context.astype(jnp.bfloat16), (largest + jnp.log(totals))[..., 0])


def backward_block(
    query_block, segment_block, context_grad, log_total, key_rows, value_rows, segments
):
    scores, allowed = masked_scores(query_block, segment_block, key_rows, segments)
    probs = jnp.exp(scores - log_total[..., None])
    prob_grad = jnp.einsum(
        "qhd,khd->hqk", context_grad, value_rows, preferred_element_type=jnp.float32
    )
    centre = jnp.sum(probs * prob_grad, axis=-1, keepdims=True)
    score_grad = jnp.where(allowed, probs * (prob_grad - centre), 0.0).astype(jnp.bfloat16)
    query_grad = jnp.einsum(
        "hqk,khd->qhd", score_grad, key_rows, preferred_element_type=jnp.float32
    ) * HD ** (-0.5)
    key_grad = jnp.einsum(
        "hqk,qhd->khd", score_grad, query_block, preferred_element_type=jnp.float32
    ) * HD ** (-0.5)
    value_grad = jnp.einsum(
        "hqk,qhd->khd", probs.astype(jnp.bfloat16), context_grad, preferred_element_type=jnp.float32
    )
    return (query_grad, key_grad, value_grad)


def adamw(master, gradient, first, second, rate, decay):
    first_new = BETA_FIRST * first + (1.0 - BETA_FIRST) * gradient
    second_new = BETA_SECOND * second + (1.0 - BETA_SECOND) * gradient * gradient
    first_hat = first_new / (1.0 - BETA_FIRST**STEP)
    second_hat = second_new / (1.0 - BETA_SECOND**STEP)
    master_new = master - rate * (first_hat / (jnp.sqrt(second_hat) + ADAM_EPS) + decay * master)
    return (master_new, first_new, second_new)


def on_device(
    tokens, segment_ids, cotangent, matrices, vectors, mat_first, mat_second, vec_first, vec_second
):
    gathered_mat, gathered_vec = (
        lax.all_gather(matrices.astype(jnp.bfloat16), ("rows", "genes"), axis=1, tiled=True),
        lax.all_gather(vectors.astype(jnp.bfloat16), ("rows", "genes"), axis=1, tiled=True),
    )
    vector_low = gathered_vec.astype(jnp.float32)
    row_count, half_len, width = tokens.shape
    token_count = row_count * half_len
    gene_count = lax.axis_size("genes")
    full_len = half_len * gene_count
    head_width = width // gene_count
    local_heads = head_width // HD
    block_len = min(512, full_len)
    block_count = full_len // block_len
    head_shape = (full_len, local_heads, HD)
    w_qkv = gathered_mat[0, :, : 3 * width]
    w_out = gathered_mat[0, :, 3 * width :]
    w_up = gathered_mat[1]
    w_down = gathered_mat[2]
    token_vals = tokens.reshape(token_count, width).astype(jnp.float32)
    normed_one, norm_one_back = jax.vjp(norm_rows, token_vals, vector_low[0], vector_low[1])
    normed_low = normed_one.astype(jnp.bfloat16)
    qkv_bias = jnp.concatenate([vector_low[2], jnp.zeros((width,), jnp.float32), vector_low[3]])
    projected = jnp.dot(normed_low, w_qkv, preferred_element_type=jnp.float32) + qkv_bias
    projected = projected.astype(jnp.bfloat16).reshape(row_count, half_len, 3, width)
    by_heads = lax.all_to_all(projected, "genes", split_axis=3, concat_axis=1, tiled=True)

    def row_forward(item):
        trio, segments = item
        query_rows = trio[:, 0].reshape(head_shape)
        key_rows = trio[:, 1].reshape(head_shape)
        value_rows = trio[:, 2].reshape(head_shape)

        def block_forward(part):
            query_block, segment_block = part
            return forward_block(query_block, segment_block, key_rows, value_rows, segments)

        context, log_total = lax.map(
            block_forward,
            (
                query_rows.reshape(block_count, block_len, local_heads, HD),
                segments.reshape(block_count, block_len),
            ),
        )
        return (context.reshape(full_len, head_width), log_total)

    context_heads, log_totals = lax.map(row_forward, (by_heads, segment_ids))
    context_tokens = lax.all_to_all(context_heads, "genes", split_axis=1, concat_axis=2, tiled=True)
    flat_context = context_tokens.reshape(token_count, width)
    branch = jnp.dot(flat_context, w_out, preferred_element_type=jnp.float32)
    middle = token_vals + branch + vector_low[4]
    normed_two, norm_two_back = jax.vjp(norm_rows, middle, vector_low[5], vector_low[6])
    normed_two_low = normed_two.astype(jnp.bfloat16)
    pre_act = jnp.dot(normed_two_low, w_up, preferred_element_type=jnp.float32) + vector_low[
        7:11
    ].reshape(4 * width)
    activated, gelu_back = jax.vjp(gelu_exact, pre_act)
    act_low = activated.astype(jnp.bfloat16)
    down_out = contract_cols(act_low, w_down) + vector_low[11]
    layer_out = (middle + down_out).astype(jnp.bfloat16).reshape(row_count, half_len, width)
    grad_low = cotangent.reshape(token_count, width)
    grad_vals = grad_low.astype(jnp.float32)
    grad_down = contract_rows(grad_low, act_low)
    grad_b_down = jnp.sum(grad_vals, axis=0)
    act_grad = jnp.dot(grad_low, w_down, preferred_element_type=jnp.float32)
    (pre_grad,) = gelu_back(act_grad)
    pre_low = pre_grad.astype(jnp.bfloat16)
    grad_b_up = jnp.sum(pre_low.astype(jnp.float32), axis=0)
    grad_up = contract_rows(normed_two_low, pre_low)
    normed_two_grad = contract_cols(pre_low, w_up)
    middle_part, grad_gain_two, grad_shift_two = norm_two_back(normed_two_grad)
    middle_grad = grad_vals + middle_part
    branch_low = middle_grad.astype(jnp.bfloat16)
    grad_b_out = jnp.sum(branch_low.astype(jnp.float32), axis=0)
    context_grad_tokens = contract_cols(branch_low, w_out).astype(jnp.bfloat16)
    grad_out = contract_rows(flat_context, branch_low)
    context_grad_heads = lax.all_to_all(
        context_grad_tokens.reshape(row_count, half_len, width),
        "genes",
        split_axis=2,
        concat_axis=1,
        tiled=True,
    )

    def row_backward(item):
        trio, segments, context_grad, log_total = item
        query_rows = trio[:, 0].reshape(head_shape)
        key_rows = trio[:, 1].reshape(head_shape)
        value_rows = trio[:, 2].reshape(head_shape)

        def block_backward(carry, part):
            query_block, segment_block, grad_block, total_block = part
            query_grad, key_grad, value_grad = backward_block(
                query_block, segment_block, grad_block, total_block, key_rows, value_rows, segments
            )
            return ((carry[0] + key_grad, carry[1] + value_grad), query_grad)

        zero_heads = jnp.zeros(head_shape, jnp.float32)
        (key_sum, value_sum), query_grads = lax.scan(
            block_backward,
            (zero_heads, zero_heads),
            (
                query_rows.reshape(block_count, block_len, local_heads, HD),
                segments.reshape(block_count, block_len),
                context_grad.reshape(block_count, block_len, local_heads, HD),
                log_total,
            ),
        )
        return jnp.stack(
            [
                query_grads.reshape(full_len, head_width),
                key_sum.reshape(full_len, head_width),
                value_sum.reshape(full_len, head_width),
            ],
            1,
        ).astype(jnp.bfloat16)

    grad_heads = lax.map(row_backward, (by_heads, segment_ids, context_grad_heads, log_totals))
    grad_tokens_qkv = lax.all_to_all(grad_heads, "genes", split_axis=1, concat_axis=3, tiled=True)
    qkv_grad = grad_tokens_qkv.reshape(token_count, 3 * width)
    qkv_grad_vals = qkv_grad.astype(jnp.float32)
    grad_b_query = jnp.sum(qkv_grad_vals[:, :width], axis=0)
    grad_b_value = jnp.sum(qkv_grad_vals[:, 2 * width :], axis=0)
    grad_qkv = contract_rows(normed_low, qkv_grad)
    normed_one_grad = contract_cols(qkv_grad, w_qkv)
    input_part, grad_gain_one, grad_shift_one = norm_one_back(normed_one_grad)
    tokens_grad = (middle_grad + input_part).reshape(row_count, half_len, width)
    grad_vector = jnp.concatenate(
        [
            jnp.stack(
                [
                    grad_gain_one,
                    grad_shift_one,
                    grad_b_query,
                    grad_b_value,
                    grad_b_out,
                    grad_gain_two,
                    grad_shift_two,
                ]
            ),
            grad_b_up.reshape(4, width),
            grad_b_down[None],
        ],
        0,
    )
    grad_attention = jnp.concatenate([grad_qkv, grad_out], 1)
    matrix_shard, vector_shard = (
        lax.psum_scatter(
            jnp.stack([grad_attention, grad_up, grad_down]),
            ("rows", "genes"),
            scatter_dimension=1,
            tiled=True,
        ),
        lax.psum_scatter(grad_vector, ("rows", "genes"), scatter_dimension=1, tiled=True),
    )
    matrices_new, matrices_first, matrices_second = adamw(
        matrices, matrix_shard, mat_first, mat_second, MATRIX_RATE, MATRIX_DECAY
    )
    vectors_new, vectors_first, vectors_second = adamw(
        vectors, vector_shard, vec_first, vec_second, VECTOR_RATE, 0.0
    )
    return (
        layer_out,
        tokens_grad,
        matrices_new,
        matrices_first,
        matrices_second,
        vectors_new,
        vectors_first,
        vectors_second,
    )


def solution(mesh):
    in_specs = (
        P("rows", "genes", None),
        P("rows", None),
        P("rows", "genes", None),
        P(None, ("rows", "genes"), None),
        P(None, ("rows", "genes")),
        P(None, ("rows", "genes"), None),
        P(None, ("rows", "genes"), None),
        P(None, ("rows", "genes")),
        P(None, ("rows", "genes")),
    )
    out_specs = (
        P("rows", "genes", None),
        P("rows", "genes", None),
        P(None, ("rows", "genes"), None),
        P(None, ("rows", "genes"), None),
        P(None, ("rows", "genes"), None),
        P(None, ("rows", "genes")),
        P(None, ("rows", "genes")),
        P(None, ("rows", "genes")),
    )
    return jax.shard_map(
        on_device, mesh=mesh, in_specs=in_specs, out_specs=out_specs, check_vma=False
    )
```

profile of v0, /device:TPU:0, one launch (start us, length us, event | category | flops | bytes accessed | tf_op | source)
XLA Modules:
  0.0 1311.0 jit_solution(17988636091185154317)
XLA Ops:
  11.2 44.6 %all-gather = bf16[32,24,12]{1,2,0:T(8,128)(2,1)S(1)} all-gather(bf16[1,24,12]{1,2,0:T(8,128)(2,1)S(1)} %convert_bitcast_fusion.1), channel_id=1, replica_groups=mesh['rows'=16,'genes'=2] {'rows','genes'}, dimensions={0}, use_global_device_ids=true | all-gather | bytes 19008 | tf_op jit(solution)/shard_map/all_gather | solution.py:96
  61.1 56.0 %all-gather.3.cloned.1.call-done = bf16[3,768,3072]{2,1,0:T(8,128)(2,1)} async-done(((bf16[3,24,3072]{2,1,0:T(8,128)(2,1)}), bf16[3,768,3072]{2,1,0:T(8,128)(2,1)}) %all-gather.3.cloned.1.call-update) | async-done | bytes 14155792 | tf_op jit(solution)/shard_map/all_gather | solution.py:95
  170.2 148.0 %while.45 = (s32[]{:T(128)}, bf16[4,512,6,64]{1,3,2,0:T(8,128)(2,1)}, f32[4,6,512]{2,1,0:T(8,128)}, s32[4,512]{1,0:T(4,128)S(1)}, s32[2048]{0:T(1024)S(1)}, /*in...) while((s32[]{:T(128)}, ...), condition=%wide.region_5.6_spmd, body=%wide.region_2.5_spmd.sunk | while | flops 1687352320 | bytes 83742304 | solution.py:130
  170.9 11.5 fusion.135
  182.4 12.0 fusion.136
  194.9 12.2 fusion.137
  207.9 11.5 fusion.135
  219.4 12.0 fusion.136
  231.9 12.2 fusion.137
  244.9 11.5 fusion.135
  256.4 12.0 fusion.136
  268.9 12.2 fusion.137
  281.8 11.5 fusion.135
  293.3 12.0 fusion.136
  305.9 12.2 fusion.137
  335.8 34.5 %reduce.21 = bf16[2048,384]{1,0:T(8,128)(2,1)S(1)} reduce(bf16[2048,1,384]{2,1,0:T(2,128)(2,1)} %bitcast.230, bf16[]{:T(256)} %broadcast.293), dimensions={1}, to_apply=%bitcast.151.reduce_sub_computation | reduce | bytes 3145730
  386.4 38.6 %multiply_convert_fusion = (bf16[1024,3072]{1,0:T(8,128)(2,1)}, f32[1024,3072]{1,0:T(8,128)}, f32[1024,3072]{1,0:T(8,128)}) fusion(f32[3072]{0:T(1024)S(1)} %copy-done.45, bf16[3,768,3072]{2,1,0:T(8,128)(2,1)} %all-gather.3.cloned.1.call-done, f32[1024,768]{0,1:T(8,128)S(1)} %get-tuple-element.426, f32[768]{0:T(1024)S(1)} %copy-done.51, ...), kind=kOutput, calls=%fused_computation.55 | convolution fusion | flops 5043388416 | bytes 39348224 | tf_op jit(solution)/shard_map/dot_general | solution.py:146
  425.0 17.5 %convert_reduce_fusion = (f32[3072]{0:T(1024)}, bf16[1024,3072]{1,0:T(8,128)(2,1)}) fusion(f32[1024,3072]{1,0:T(8,128)} %get-tuple-element.417, bf16[3,768,3072]{2,1,0:T(8,128)(2,1)} %all-gather.3.cloned.1.call-done, bf16[1,1024,768]{2,1,0:T(8,128)(2,1)S(1)} %copy-done.21, f32[1024,3072]{1,0:T(8,128)} %get-tuple-element.427, f32[3072]{0:T(1024)S(1)} %copy-done.45), kind=kOutput, calls=%fused_computation.53 | convolution fusion | flops 4885312512 | bytes 37773312 | tf_op jit(solution)/shard_map/dot_general | solution.py:157
  442.5 10.7 convolution_bitcast_fusion.1
  487.7 11.0 reduce.22
  521.1 430.0 %while.46 = (s32[]{:T(128)}, f32[2048,6,64]{0,2,1:T(8,128)}, f32[2048,6,64]{0,2,1:T(8,128)}, bf16[4,512,6,64]{1,3,2,0:T(8,128)(2,1)}, bf16[4,512,6,64]{1,3,2,0:T...) while((s32[]{:T(128)}, f32[2048,6,64]{0,2,1:T(8,128)}, ...), condition=%wide.region_12.13_spmd.clone, body=%wide.region_10.12_spmd.clone.sunk | while | flops 4119799808 | bytes 304927392 | solution.py:191
  523.2 12.6 subtract_exponential_fusion.3
  535.9 11.0 fusion.148
  546.9 34.6 %bitcast_add_fusion.4 = f32[2048,6,64]{0,2,1:T(8,128)} fusion(f32[2048,6,64]{0,2,1:T(8,128)} %get-tuple-element.595, f32[6,512,2048]{2,1,0:T(8,128)} %subtract_exponential_fusion.3, f32[6,512,2048]{2,1,0:T(8,128)} %fusion.148, pred[512,2048]{1,0:T(8,128)(4,1)} %copy-done.16, pred[]{:T(512)S(6)} %compare.3, ...), kind=kOutput, calls=%fused_computation.28.clone.1 | convolution fusion | flops 839128064 | bytes 108397056 | tf_op jit(solution)/shard_map/while/body/eval_jaxpr/while/body/eval_jaxpr/hqk,qhd->khd/dot_general | solution.py:73
  581.5 33.5 %fusion.149 = bf16[4,512,6,64]{1,3,2,0:T(8,128)(2,1)} fusion(bf16[4,512,6,64]{1,3,2,0:T(8,128)(2,1)} %get-tuple-element.597, s32[]{:T(128)} %get-tuple-element.594, bf16[2048,6,64]{0,2,1:T(8,128)(2,1)S(1)} %get-tuple-element.614, f32[6,512,2048]{2,1,0:T(8,128)} %subtract_exponential_fusion.3, f32[6,512,2048]{2,1,0:T(8,128)} %fusion.148, ...), kind=kOutput, calls=%fused_computation.32.clone.1 | convolution fusion | flops 836965376 | bytes 104071680 | tf_op jit(solution)/shard_map/while/body/eval_jaxpr/while/body/eval_jaxpr/hqk,khd->qhd/dot_general | solution.py:70
  615.0 12.3 bitcast_add_fusion.5
  629.4 12.6 subtract_exponential_fusion.3
  642.0 11.0 fusion.148
  653.1 35.5 %bitcast_add_fusion.4 = f32[2048,6,64]{0,2,1:T(8,128)} fusion(f32[2048,6,64]{0,2,1:T(8,128)} %get-tuple-element.595, f32[6,512,2048]{2,1,0:T(8,128)} %subtract_exponential_fusion.3, f32[6,512,2048]{2,1,0:T(8,128)} %fusion.148, pred[512,2048]{1,0:T(8,128)(4,1)} %copy-done.16, pred[]{:T(512)S(6)} %compare.3, ...), kind=kOutput, calls=%fused_computation.28.clone.1 | convolution fusion | flops 839128064 | bytes 108397056 | tf_op jit(solution)/shard_map/while/body/eval_jaxpr/while/body/eval_jaxpr/hqk,qhd->khd/dot_general | solution.py:73
  688.6 33.5 %fusion.149 = bf16[4,512,6,64]{1,3,2,0:T(8,128)(2,1)} fusion(bf16[4,512,6,64]{1,3,2,0:T(8,128)(2,1)} %get-tuple-element.597, s32[]{:T(128)} %get-tuple-element.594, bf16[2048,6,64]{0,2,1:T(8,128)(2,1)S(1)} %get-tuple-element.614, f32[6,512,2048]{2,1,0:T(8,128)} %subtract_exponential_fusion.3, f32[6,512,2048]{2,1,0:T(8,128)} %fusion.148, ...), kind=kOutput, calls=%fused_computation.32.clone.1 | convolution fusion | flops 836965376 | bytes 104071680 | tf_op jit(solution)/shard_map/while/body/eval_jaxpr/while/body/eval_jaxpr/hqk,khd->qhd/dot_general | solution.py:70
  722.0 13.2 %bitcast_add_fusion.5 = f32[2048,6,64]{0,2,1:T(8,128)} fusion(f32[2048,6,64]{0,2,1:T(8,128)} %get-tuple-element.596, f32[6,512,2048]{2,1,0:T(8,128)} %subtract_exponential_fusion.3, pred[]{:T(512)S(6)} %compare.3, bf16[4,512,6,64]{1,3,2,0:T(8,128)(2,1)} %get-tuple-element.616, s32[]{:T(128)} %get-tuple-element.594), kind=kOutput, calls=%fused_computation.27.clone.1 | convolution fusion | flops 813170688 | bytes 31851008 | tf_op jit(solution)/shard_map/while/body/eval_jaxpr/while/body/eval_jaxpr/hqk,qhd->khd/dot_general | solution.py:76
  737.3 12.6 subtract_exponential_fusion.3
  750.0 11.0 fusion.148
  761.0 35.6 %bitcast_add_fusion.4 = f32[2048,6,64]{0,2,1:T(8,128)} fusion(f32[2048,6,64]{0,2,1:T(8,128)} %get-tuple-element.595, f32[6,512,2048]{2,1,0:T(8,128)} %subtract_exponential_fusion.3, f32[6,512,2048]{2,1,0:T(8,128)} %fusion.148, pred[512,2048]{1,0:T(8,128)(4,1)} %copy-done.16, pred[]{:T(512)S(6)} %compare.3, ...), kind=kOutput, calls=%fused_computation.28.clone.1 | convolution fusion | flops 839128064 | bytes 108397056 | tf_op jit(solution)/shard_map/while/body/eval_jaxpr/while/body/eval_jaxpr/hqk,qhd->khd/dot_general | solution.py:73
  796.6 33.5 %fusion.149 = bf16[4,512,6,64]{1,3,2,0:T(8,128)(2,1)} fusion(bf16[4,512,6,64]{1,3,2,0:T(8,128)(2,1)} %get-tuple-element.597, s32[]{:T(128)} %get-tuple-element.594, bf16[2048,6,64]{0,2,1:T(8,128)(2,1)S(1)} %get-tuple-element.614, f32[6,512,2048]{2,1,0:T(8,128)} %subtract_exponential_fusion.3, f32[6,512,2048]{2,1,0:T(8,128)} %fusion.148, ...), kind=kOutput, calls=%fused_computation.32.clone.1 | convolution fusion | flops 836965376 | bytes 104071680 | tf_op jit(solution)/shard_map/while/body/eval_jaxpr/while/body/eval_jaxpr/hqk,khd->qhd/dot_general | solution.py:70
  830.0 13.2 %bitcast_add_fusion.5 = f32[2048,6,64]{0,2,1:T(8,128)} fusion(f32[2048,6,64]{0,2,1:T(8,128)} %get-tuple-element.596, f32[6,512,2048]{2,1,0:T(8,128)} %subtract_exponential_fusion.3, pred[]{:T(512)S(6)} %compare.3, bf16[4,512,6,64]{1,3,2,0:T(8,128)(2,1)} %get-tuple-element.616, s32[]{:T(128)} %get-tuple-element.594), kind=kOutput, calls=%fused_computation.27.clone.1 | convolution fusion | flops 813170688 | bytes 31851008 | tf_op jit(solution)/shard_map/while/body/eval_jaxpr/while/body/eval_jaxpr/hqk,qhd->khd/dot_general | solution.py:76
  845.3 12.6 subtract_exponential_fusion.3
  857.9 11.0 fusion.148
  869.0 35.5 %bitcast_add_fusion.4 = f32[2048,6,64]{0,2,1:T(8,128)} fusion(f32[2048,6,64]{0,2,1:T(8,128)} %get-tuple-element.595, f32[6,512,2048]{2,1,0:T(8,128)} %subtract_exponential_fusion.3, f32[6,512,2048]{2,1,0:T(8,128)} %fusion.148, pred[512,2048]{1,0:T(8,128)(4,1)} %copy-done.16, pred[]{:T(512)S(6)} %compare.3, ...), kind=kOutput, calls=%fused_computation.28.clone.1 | convolution fusion | flops 839128064 | bytes 108397056 | tf_op jit(solution)/shard_map/while/body/eval_jaxpr/while/body/eval_jaxpr/hqk,qhd->khd/dot_general | solution.py:73
  904.4 33.5 %fusion.149 = bf16[4,512,6,64]{1,3,2,0:T(8,128)(2,1)} fusion(bf16[4,512,6,64]{1,3,2,0:T(8,128)(2,1)} %get-tuple-element.597, s32[]{:T(128)} %get-tuple-element.594, bf16[2048,6,64]{0,2,1:T(8,128)(2,1)S(1)} %get-tuple-element.614, f32[6,512,2048]{2,1,0:T(8,128)} %subtract_exponential_fusion.3, f32[6,512,2048]{2,1,0:T(8,128)} %fusion.148, ...), kind=kOutput, calls=%fused_computation.32.clone.1 | convolution fusion | flops 836965376 | bytes 104071680 | tf_op jit(solution)/shard_map/while/body/eval_jaxpr/while/body/eval_jaxpr/hqk,khd->qhd/dot_general | solution.py:70
  937.9 13.2 %bitcast_add_fusion.5 = f32[2048,6,64]{0,2,1:T(8,128)} fusion(f32[2048,6,64]{0,2,1:T(8,128)} %get-tuple-element.596, f32[6,512,2048]{2,1,0:T(8,128)} %subtract_exponential_fusion.3, pred[]{:T(512)S(6)} %compare.3, bf16[4,512,6,64]{1,3,2,0:T(8,128)(2,1)} %get-tuple-element.616, s32[]{:T(128)} %get-tuple-element.594), kind=kOutput, calls=%fused_computation.27.clone.1 | convolution fusion | flops 813170688 | bytes 31851008 | tf_op jit(solution)/shard_map/while/body/eval_jaxpr/while/body/eval_jaxpr/hqk,qhd->khd/dot_general | solution.py:76
  960.5 10.3 copy.183
  970.8 10.7 all_to_all.63
  999.8 10.4 convolution_bitcast_fusion
  1018.9 21.2 %pad_maximum_fusion = f32[3,768,3072]{2,1,0:T(8,128)} fusion(f32[1,768,3072]{2,1,0:T(8,128)} %convolution_bitcast_fusion, f32[1,768,3072]{2,1,0:T(8,128)} %convolution_bitcast_fusion.1, f32[1,768,3072]{2,1,0:T(8,128)} %maximum_bitcast_fusion), kind=kLoop, calls=%fused_computation.50 | loop fusion | flops 14155776 | bytes 56623104 | tf_op jit(solution)/shard_map/stack | solution.py:241
  1079.0 10.5 fusion.81
  1092.6 43.1 %all-reduce = f32[12,768]{1,0:T(8,128)S(1)} all-reduce(f32[12,768]{1,0:T(8,128)S(1)} %concatenate.19), channel_id=3, replica_groups=mesh['rows'=16,'genes'=2] {'rows','genes'}, use_global_device_ids=true, to_apply=%region_25.26.clone | all-reduce | flops 9216 | bytes 73728
  1136.5 164.4 %reduce-scatter.3.cloned.1.call-done = f32[3,24,3072]{2,1,0:T(8,128)} async-done(((f32[3,768,3072]{2,1,0:T(8,128)}), f32[3,24,3072]{2,1,0:T(8,128)}) %reduce-scatter.3.cloned.1.call-update) | async-done | bytes 884752 | tf_op jit(solution)/shard_map/reduce_scatter | solution.py:240
  (242 shorter events, 248.2 us)
Async XLA Ops:
  7.2 4.0 copy-start.40
  7.2 49.5 %copy-start.24 = (s32[1,2048]{1,0:T(1,128)S(1)}, s32[1,2048]{1,0:T(1,128)}, u32[]{:S(2)}) copy-start(s32[1,2048]{1,0:T(1,128)} %param.14) | copy-start | bytes 24580
  7.2 50.8 %copy-start.20 = (bf16[1,1024,768]{2,1,0:T(8,128)(2,1)S(1)}, bf16[1,1024,768]{2,1,0:T(8,128)(2,1)}, u32[]{:S(2)}) copy-start(bf16[1,1024,768]{2,1,0:T(8,128)(2,1)} %param.15) | copy-start | bytes 4718596
  7.2 109.8 %all-gather.3.cloned.1.call-start = ((), (), s32[]{:S(2)}) async-start(), calls=%async_computation.5 | async-start | bytes 14598144 | tf_op jit(solution)/shard_map/all_gather | solution.py:95
  9.4 1291.5 %reduce-scatter.3.cloned.1.call-start = ((), (), s32[]{:S(2)}) async-start(), calls=%async_computation.6 | async-start | bytes 29196288 | tf_op jit(solution)/shard_map/reduce_scatter | solution.py:240
  11.2 105.9 %copy-start.5 = (bf16[1,1024,768]{1,2,0:T(8,128)(2,1)}, bf16[1,1024,768]{1,2,0:T(8,128)(2,1)S(1)}, u32[]{:S(2)}) copy-start(bf16[1,1024,768]{1,2,0:T(8,128)(2,1)S(1)} %copy.161) | copy-start | bytes 4718596
  60.3 64.5 %copy-start.31 = (f32[768]{0:T(1024)}, f32[768]{0:T(1024)S(1)}, u32[]{:S(2)}) copy-start(f32[768]{0:T(1024)S(1)} %get-tuple-element.367) | copy-start | bytes 9220
  60.3 64.5 %copy-start.49 = (f32[768]{0:T(1024)}, f32[768]{0:T(1024)S(1)}, u32[]{:S(2)}) copy-start(f32[768]{0:T(1024)S(1)} %get-tuple-element.366) | copy-start | bytes 9220
  60.6 64.2 %copy-start.28 = (f32[1024]{0:T(1024)}, f32[1024]{0:T(1024)S(1)}, u32[]{:S(2)}) copy-start(f32[1024]{0:T(1024)S(1)} %broadcast_multiply_fusion.1) | copy-start | bytes 12292
  61.1 63.8 %copy-start.37 = (f32[1024]{0:T(1024)}, f32[1024]{0:T(1024)S(1)}, u32[]{:S(2)}) copy-start(f32[1024]{0:T(1024)S(1)} %fusion.67) | copy-start | bytes 12292
  61.1 63.8 %copy-start.33 = (f32[1024]{0:T(1024)}, f32[1024]{0:T(1024)S(1)}, u32[]{:S(2)}) copy-start(f32[1024]{0:T(1024)S(1)} %fusion.86) | copy-start | bytes 12292
  318.2 8.7 copy-start
  318.2 8.7 copy-start.3
  318.2 8.7 copy-start.30
  378.3 3.9 copy-start.6
  378.3 3.9 copy-start.52
  385.6 56.9 %copy-start.9 = (f32[1024,768]{0,1:T(8,128)}, f32[1024,768]{0,1:T(8,128)S(1)}, u32[]{:S(2)}) copy-start(f32[1024,768]{0,1:T(8,128)S(1)} %get-tuple-element.426) | copy-start | bytes 9437188
  386.4 38.6 %copy-start.21 = (bf16[1,1024,768]{2,1,0:T(8,128)(2,1)S(1)}, bf16[1,1024,768]{2,1,0:T(8,128)(2,1)}, u32[]{:S(2)}) copy-start(bf16[1,1024,768]{2,1,0:T(8,128)(2,1)} %param.15) | copy-start | bytes 4718596
  442.5 10.7 copy-start.54
  462.9 3.7 copy-start.10
  466.6 3.5 copy-start.14
  512.9 8.2 copy-start.1
  512.9 8.2 copy-start.4
  512.9 8.2 copy-start.25
  522.5 13.4 %copy-start.16 = (pred[512,2048]{1,0:T(8,128)(4,1)}, pred[512,2048]{1,0:T(8,128)(4,1)S(1)}, u32[]{:S(2)}) copy-start(pred[512,2048]{1,0:T(8,128)(4,1)S(1)} %broadcast_compare_fusion.5) | copy-start | bytes 3145732 | tf_op jit(solution)/shard_map/while/body/eval_jaxpr/while
  628.6 13.4 %copy-start.16 = (pred[512,2048]{1,0:T(8,128)(4,1)}, pred[512,2048]{1,0:T(8,128)(4,1)S(1)}, u32[]{:S(2)}) copy-start(pred[512,2048]{1,0:T(8,128)(4,1)S(1)} %broadcast_compare_fusion.5) | copy-start | bytes 3145732 | tf_op jit(solution)/shard_map/while/body/eval_jaxpr/while
  736.6 13.4 %copy-start.16 = (pred[512,2048]{1,0:T(8,128)(4,1)}, pred[512,2048]{1,0:T(8,128)(4,1)S(1)}, u32[]{:S(2)}) copy-start(pred[512,2048]{1,0:T(8,128)(4,1)S(1)} %broadcast_compare_fusion.5) | copy-start | bytes 3145732 | tf_op jit(solution)/shard_map/while/body/eval_jaxpr/while
  844.6 13.4 %copy-start.16 = (pred[512,2048]{1,0:T(8,128)(4,1)}, pred[512,2048]{1,0:T(8,128)(4,1)S(1)}, u32[]{:S(2)}) copy-start(pred[512,2048]{1,0:T(8,128)(4,1)S(1)} %broadcast_compare_fusion.5) | copy-start | bytes 3145732 | tf_op jit(solution)/shard_map/while/body/eval_jaxpr/while
  954.9 2.8 copy-start.2
  984.2 6.8 copy-start.7
  984.2 6.8 copy-start.29
  984.2 6.8 copy-start.32
  984.2 6.8 copy-start.34
  984.2 6.8 copy-start.50
  991.0 8.7 copy-start.22
  1061.9 3.0 copy-start.38
  1061.9 3.6 copy-start.8
  1064.9 3.0 copy-start.18
  1064.9 3.0 copy-start.36
  1067.9 5.9 copy-start.15
  1074.6 4.4 copy-start.11
  1074.6 4.4 copy-start.48
  1089.5 46.2 %copy-start.41 = (f32[12,24]{1,0:T(8,128)S(1)}, f32[12,24]{1,0:T(8,128)}, u32[]{:S(2)}) copy-start(f32[12,24]{1,0:T(8,128)} %param.17) | copy-start | bytes 3460
  1089.5 46.2 %copy-start.46 = (f32[12,24]{1,0:T(8,128)S(1)}, f32[12,24]{1,0:T(8,128)}, u32[]{:S(2)}) copy-start(f32[12,24]{1,0:T(8,128)} %param.20) | copy-start | bytes 3460
  1089.5 46.2 %copy-start.47 = (f32[12,24]{1,0:T(8,128)S(1)}, f32[12,24]{1,0:T(8,128)}, u32[]{:S(2)}) copy-start(f32[12,24]{1,0:T(8,128)} %param.21) | copy-start | bytes 3460
  1089.5 211.3 %copy-start.19 = (f32[3,24,3072]{2,1,0:T(8,128)S(1)}, f32[3,24,3072]{2,1,0:T(8,128)}, u32[]{:S(2)}) copy-start(f32[3,24,3072]{2,1,0:T(8,128)} %param.16) | copy-start | bytes 2654212
  1089.6 211.3 %copy-start.26 = (f32[3,24,3072]{2,1,0:T(8,128)S(1)}, f32[3,24,3072]{2,1,0:T(8,128)}, u32[]{:S(2)}) copy-start(f32[3,24,3072]{2,1,0:T(8,128)} %param.18) | copy-start | bytes 2654212
  1089.6 211.3 %copy-start.27 = (f32[3,24,3072]{2,1,0:T(8,128)S(1)}, f32[3,24,3072]{2,1,0:T(8,128)}, u32[]{:S(2)}) copy-start(f32[3,24,3072]{2,1,0:T(8,128)} %param.19) | copy-start | bytes 2654212
  (12 other events, 14.3 us)
Sparse Core Ops, SparseCore 0:
  11.5 105.4 all-gather.2
  1040.2 260.5 reduce-scatter.2
where the time goes:
time: 1320 us; the launch traced here: 1310 us
  matrix products  650 us (49%)
  waiting for transfers between devices  220 us (17%)
  other arithmetic  165 us (12%)
  local copies, waits for them, and re-layouts  142 us (11%)
  blocking collectives  118 us (9%)
  between operations  14.9 us (1%)
    reduce_scatter x1, waiting for transfers between devices, on_device(): lax.psum_scatter(jnp.stack([grad_attention, grad_up, grad_down]), ('rows'...  164 us
    dot_general x4, matrix products, backward_block(): jnp.einsum('hqk,qhd->khd', score_grad, query_block, preferred_element_typ...  141 us
    dot_general x4, matrix products, backward_block(): jnp.einsum('hqk,khd->qhd', score_grad, key_rows, preferred_element_type=j...  134 us
    dot_general x8, matrix products, masked_scores(): jnp.einsum('qhd,khd->hqk', query_block, key_rows, preferred_element_type=...  96.5 us
    all_gather x1, waiting for transfers between devices, on_device(): lax.all_gather(matrices.astype(jnp.bfloat16), ('rows', 'genes'), axis=1,...  56 us
    dot_general x4, matrix products, backward_block(): jnp.einsum('hqk,qhd->khd', probs.astype(jnp.bfloat16), context_grad, pref...  51.8 us
    dot_general x4, matrix products, forward_block(): jnp.einsum('hqk,khd->qhd', probs_low, value_rows, preferred_element_type=...  49 us
    reduce_sum x4, other arithmetic, forward_block(): totals = jnp.sum(weights, axis=-1, keepdims=True)  47.8 us
  transfers between devices with their start and end apart: 2, of which 2 were waited for; matrix products, arithmetic and copies ran while one was open for 4% of the time, Pallas kernels for 0%

commit v1 on v0

v1 whole, which is shorter than its diff:
```python
import jax
import jax.numpy as jnp
from jax import lax
from jax.experimental import pallas as pl
from jax.experimental.pallas import tpu as pltpu
from jax.sharding import PartitionSpec as P

HD = 64
STEP = 10
CELL_MAX = 512

BETA_FIRST = 0.5
BETA_SECOND = 0.5
ADAM_EPS = 1e-08
MATRIX_RATE = 0.05
VECTOR_RATE = 0.3
MATRIX_DECAY = 0.01
NORM_EPS = 1e-05
SCORE_MASK = -1e30
PAIR = 2 * HD
QBLK = 256
KBLK = 256
VEC_COLS = 128

F32 = jnp.float32
BF16 = jnp.bfloat16


def contract_rows(former, latter):
    return lax.dot_general(
        former, latter, (((0,), (0,)), ((), ())), preferred_element_type=jnp.float32
    )


def contract_cols(former, latter):
    return lax.dot_general(
        former, latter, (((1,), (1,)), ((), ())), preferred_element_type=jnp.float32
    )


def matmul(former, latter):
    return lax.dot_general(
        former, latter, (((1,), (0,)), ((), ())), preferred_element_type=jnp.float32
    )


def norm_stats(values):
    centre = values - jnp.mean(values, axis=-1, keepdims=True)
    spread = jnp.mean(centre * centre, axis=-1, keepdims=True)
    factor = lax.rsqrt(spread + NORM_EPS)
    return centre * factor, factor


def norm_back(grad, hat, factor, gain):
    scaled = grad * gain
    mean_one = jnp.mean(scaled, axis=-1, keepdims=True)
    mean_two = jnp.mean(scaled * hat, axis=-1, keepdims=True)
    return factor * (scaled - mean_one - hat * mean_two)


def normal_parts(values):
    bell = jnp.exp(-0.5 * values * values)
    t = 1.0 / (1.0 + 0.3275911 * 0.7071067811865476 * jnp.abs(values))
    poly = t * (
        0.254829592
        + t * (-0.284496736 + t * (1.421413741 + t * (-1.453152027 + t * 1.061405429)))
    )
    tail = 0.5 * poly * bell
    return jnp.where(values < 0.0, tail, 1.0 - tail), 0.3989422804014327 * bell


def split_pair(block):
    lane = lax.broadcasted_iota(jnp.int32, block.shape, 1)
    zero = jnp.zeros_like(block)
    return jnp.concatenate(
        [jnp.where(lane < HD, block, zero), jnp.where(lane < HD, zero, block)], 0
    )


def tile_lanes(block, times):
    return jnp.concatenate([block] * times, 1)


def attn_forward_kernel(
    table, q_ref, k_ref, v_ref, kh_ref, vh_ref, segq_ref, segk_ref, ctx_ref, lse_ref, k_all, v_turn
):
    own = k_ref.shape[0]
    halo = kh_ref.shape[0]
    k_all[:own, :] = k_ref[...]
    k_all[own:, :] = kh_ref[...]
    for b in range(own // KBLK):
        v_turn[b] = v_ref[b * KBLK : (b + 1) * KBLK, :].T
    for b in range(halo // KBLK):
        v_turn[own // KBLK + b] = vh_ref[b * KBLK : (b + 1) * KBLK, :].T
    for i in range(own // QBLK):
        rows = slice(i * QBLK, (i + 1) * QBLK)
        queries = split_pair(q_ref[rows, :] * BF16(HD**-0.5))
        seg_q = tile_lanes(segq_ref[:, rows], 2)

        def step(j, carry):
            largest, total, acc_a, acc_b = carry
            b = table[i, j + 1]
            at = pl.ds(pl.multiple_of(b * KBLK, KBLK), KBLK)
            scores = contract_cols(k_all[at, :], queries)
            allowed = tile_lanes(segk_ref[at, :], 2 * QBLK // 128) == seg_q
            scores = jnp.where(allowed, scores, SCORE_MASK)
            new_largest = jnp.maximum(largest, jnp.max(scores, axis=0, keepdims=True))
            weights = jnp.exp(scores - new_largest)
            shrink = jnp.exp(largest - new_largest)
            total = total * shrink + jnp.sum(weights, axis=0, keepdims=True)
            low = weights.astype(BF16)
            acc_a = acc_a * shrink[:, :QBLK] + matmul(v_turn[b, :HD, :], low[:, :QBLK])
            acc_b = acc_b * shrink[:, QBLK:] + matmul(v_turn[b, HD:, :], low[:, QBLK:])
            return new_largest, total, acc_a, acc_b

        start = (
            jnp.full((1, 2 * QBLK), SCORE_MASK, F32),
            jnp.zeros((1, 2 * QBLK), F32),
            jnp.zeros((HD, QBLK), F32),
            jnp.zeros((HD, QBLK), F32),
        )
        largest, total, acc_a, acc_b = lax.fori_loop(0, table[i, 0], step, start)
        inverse = 1.0 / total
        context = jnp.concatenate([acc_a * inverse[:, :QBLK], acc_b * inverse[:, QBLK:]], 0)
        ctx_ref[rows, :] = context.T.astype(BF16)
        lse = largest + jnp.log(total)
        lse_ref[0, 0:1, rows] = lse[:, :QBLK]
        lse_ref[0, 1:2, rows] = lse[:, QBLK:]


def attn_backward_kernel(
    table,
    q_ref,
    k_ref,
    v_ref,
    kh_ref,
    vh_ref,
    segq_ref,
    segk_ref,
    grad_ref,
    ctx_ref,
    lse_ref,
    dq_ref,
    dk_ref,
    dv_ref,
    dh_ref,
    k_all,
    v_all,
    k_turn,
    dk_all,
    dv_all,
):
    own = k_ref.shape[0]
    halo = kh_ref.shape[0]
    k_all[:own, :] = k_ref[...]
    k_all[own:, :] = kh_ref[...]
    v_all[:own, :] = v_ref[...]
    v_all[own:, :] = vh_ref[...]
    for b in range((own + halo) // KBLK):
        k_turn[b] = k_all[b * KBLK : (b + 1) * KBLK, :].T
    dk_all[...] = jnp.zeros_like(dk_all)
    dv_all[...] = jnp.zeros_like(dv_all)
    for i in range(own // QBLK):
        rows = slice(i * QBLK, (i + 1) * QBLK)
        queries = split_pair(q_ref[rows, :] * BF16(HD**-0.5))
        grads = split_pair(grad_ref[rows, :])
        seg_q = tile_lanes(segq_ref[:, rows], 2)
        turned = (grad_ref[rows, :].astype(F32) * ctx_ref[rows, :].astype(F32)).T
        centre = jnp.concatenate(
            [
                jnp.sum(turned[:HD], axis=0, keepdims=True),
                jnp.sum(turned[HD:], axis=0, keepdims=True),
            ],
            1,
        )
        lse = jnp.concatenate([lse_ref[0, 0:1, rows], lse_ref[0, 1:2, rows]], 1)

        def step(j, carry):
            acc_a, acc_b = carry
            b = table[i, j + 1]
            at = pl.ds(pl.multiple_of(b * KBLK, KBLK), KBLK)
            scores = contract_cols(k_all[at, :], queries)
            allowed = tile_lanes(segk_ref[at, :], 2 * QBLK // 128) == seg_q
            probs = jnp.exp(jnp.where(allowed, scores - lse, SCORE_MASK))
            prob_grad = contract_cols(v_all[at, :], grads)
            score_grad = (probs * (prob_grad - centre)).astype(BF16)
            dv_all[at, :] += matmul(probs.astype(BF16), grads)
            dk_all[at, :] += matmul(score_grad, queries)
            acc_a = acc_a + matmul(k_turn[b, :HD, :], score_grad[:, :QBLK])
            acc_b = acc_b + matmul(k_turn[b, HD:, :], score_grad[:, QBLK:])
            return acc_a, acc_b

        start = (jnp.zeros((HD, QBLK), F32), jnp.zeros((HD, QBLK), F32))
        acc_a, acc_b = lax.fori_loop(0, table[i, 0], step, start)
        dq_ref[rows, :] = (jnp.concatenate([acc_a, acc_b], 0) * HD**-0.5).T.astype(BF16)
    dk_ref[...] = dk_all[:own, :].astype(BF16)
    dv_ref[...] = dv_all[:own, :].astype(BF16)
    dh_ref[0] = dk_all[own:, :].astype(BF16)
    dh_ref[1] = dv_all[own:, :].astype(BF16)


def block_table(seg_own, seg_halo):
    first = seg_own[::QBLK][:, None]
    last = seg_own[QBLK - 1 :: QBLK][:, None]

    def bounds(segments):
        below = jnp.sum((segments[None, :] < first).astype(jnp.int32), axis=1)
        upto = jnp.sum((segments[None, :] <= last).astype(jnp.int32), axis=1)
        return below // KBLK, (upto + KBLK - 1) // KBLK

    low, high = bounds(seg_own)
    halo_low, halo_high = bounds(seg_halo)
    own_count = high - low
    count = own_count + halo_high - halo_low
    index = jnp.arange((seg_own.shape[0] + seg_halo.shape[0]) // KBLK, dtype=jnp.int32)[None, :]
    own_blocks = seg_own.shape[0] // KBLK
    blocks = jnp.where(
        index < own_count[:, None],
        low[:, None] + index,
        own_blocks + halo_low[:, None] + index - own_count[:, None],
    )
    return jnp.concatenate([count[:, None], blocks], 1)


def attention_specs(own, halo, pairs):
    def column(length, start):
        return pl.BlockSpec((length, PAIR), lambda p, t: (0, start + p))

    def whole(shape):
        return pl.BlockSpec(shape, lambda p, t: (0,) * len(shape))

    return [
        column(own, 0),
        column(own, pairs),
        column(own, 2 * pairs),
        column(halo, 0),
        column(halo, pairs),
        whole((1, own)),
        whole((own + halo, 128)),
    ], column


def attention_forward(table, qkv, halo_kv, seg_row, seg_keys):
    own, width = qkv.shape[0], qkv.shape[1] // 3
    halo = halo_kv.shape[0]
    pairs = width // PAIR
    specs, column = attention_specs(own, halo, pairs)
    return pl.pallas_call(
        attn_forward_kernel,
        grid_spec=pltpu.PrefetchScalarGridSpec(
            num_scalar_prefetch=1,
            grid=(pairs,),
            in_specs=specs,
            out_specs=[column(own, 0), pl.BlockSpec((1, 2, own), lambda p, t: (p, 0, 0))],
            scratch_shapes=[
                pltpu.VMEM((own + halo, PAIR), BF16),
                pltpu.VMEM(((own + halo) // KBLK, PAIR, KBLK), BF16),
            ],
        ),
        out_shape=[
            jax.ShapeDtypeStruct((own, width), BF16),
            jax.ShapeDtypeStruct((pairs, 2, own), F32),
        ],
        name="attn_forward",
    )(table, qkv, qkv, qkv, halo_kv, halo_kv, seg_row, seg_keys)


def attention_backward(table, qkv, halo_kv, seg_row, seg_keys, grad, context, lse):
    own, width = qkv.shape[0], qkv.shape[1] // 3
    halo = halo_kv.shape[0]
    pairs = width // PAIR
    specs, column = attention_specs(own, halo, pairs)
    low = jax.ShapeDtypeStruct((own, width), BF16)
    return pl.pallas_call(
        attn_backward_kernel,
        grid_spec=pltpu.PrefetchScalarGridSpec(
            num_scalar_prefetch=1,
            grid=(pairs,),
            in_specs=specs
            + [column(own, 0), column(own, 0), pl.BlockSpec((1, 2, own), lambda p, t: (p, 0, 0))],
            out_specs=[column(own, 0)] * 3
            + [pl.BlockSpec((2, halo, PAIR), lambda p, t: (0, 0, p))],
            scratch_shapes=[
                pltpu.VMEM((own + halo, PAIR), BF16),
                pltpu.VMEM((own + halo, PAIR), BF16),
                pltpu.VMEM(((own + halo) // KBLK, PAIR, KBLK), BF16),
                pltpu.VMEM((own + halo, PAIR), F32),
                pltpu.VMEM((own + halo, PAIR), F32),
            ],
        ),
        out_shape=[low, low, low, jax.ShapeDtypeStruct((2, halo, width), BF16)],
        name="attn_backward",
    )(table, qkv, qkv, qkv, halo_kv, halo_kv, seg_row, seg_keys, grad, context, lse)


def adamw(master, gradient, first, second, rate, decay):
    first_new = BETA_FIRST * first + (1.0 - BETA_FIRST) * gradient
    second_new = BETA_SECOND * second + (1.0 - BETA_SECOND) * gradient * gradient
    first_hat = first_new / (1.0 - BETA_FIRST**STEP)
    second_hat = second_new / (1.0 - BETA_SECOND**STEP)
    master_new = master - rate * (first_hat / (jnp.sqrt(second_hat) + ADAM_EPS) + decay * master)
    return (master_new, first_new, second_new)


BOTH = ("rows", "genes")
SWAP = [(0, 1), (1, 0)]


def gather_rows(shard):
    return lax.all_gather(shard, BOTH, axis=0, tiled=True)


def scatter_rows(whole):
    return lax.psum_scatter(whole, BOTH, scatter_dimension=0, tiled=True).astype(F32)


def on_device(
    tokens, segment_ids, cotangent, matrices, vectors, mat_first, mat_second, vec_first, vec_second
):
    row_count, own, width = tokens.shape
    hidden = matrices.shape[2]
    vec_rows = vectors.shape[0]
    halo = min(CELL_MAX, own)
    core = lax.axis_index("genes")
    mat_low = matrices.astype(BF16)
    vec_low = jnp.pad(vectors.astype(BF16).T, ((0, 0), (0, VEC_COLS - vec_rows)))
    first_part = gather_rows(jnp.concatenate([mat_low[0, :, : 3 * width], vec_low], 1))
    second_part = gather_rows(
        jnp.concatenate([mat_low[1], mat_low[2], mat_low[0, :, 3 * width :]], 1)
    )
    w_qkv = first_part[:, : 3 * width]
    vec = first_part[:, 3 * width : 3 * width + vec_rows].T.astype(F32)
    w_up = second_part[:, :hidden]
    w_down = second_part[:, hidden : 2 * hidden]
    w_out = second_part[:, 2 * hidden :]

    x = tokens.reshape(own, width).astype(F32)
    hat_one, factor_one = norm_stats(x)
    n1 = (hat_one * vec[0] + vec[1]).astype(BF16)
    qkv_bias = jnp.concatenate([vec[2], jnp.zeros((width,), F32), vec[3]])
    qkv = (matmul(n1, w_qkv) + qkv_bias).astype(BF16)

    segments = segment_ids.reshape(-1)
    seg_own = lax.dynamic_slice_in_dim(segments, core * own, own)
    halo_start = jnp.where(core == 0, own, own - halo)
    seg_halo = lax.dynamic_slice_in_dim(segments, halo_start, halo)
    table = block_table(seg_own, seg_halo)
    seg_row = seg_own[None, :]
    seg_keys = jnp.broadcast_to(jnp.concatenate([seg_own, seg_halo])[:, None], (own + halo, 128))
    send_start = jnp.where(core == 0, own - halo, 0)
    halo_kv = lax.ppermute(
        lax.dynamic_slice(qkv, (send_start, width), (halo, 2 * width)), "genes", SWAP
    )
    ctx, lse = attention_forward(table, qkv, halo_kv, seg_row, seg_keys)

    x2 = x + matmul(ctx, w_out) + vec[4]
    hat_two, factor_two = norm_stats(x2)
    n2 = (hat_two * vec[5] + vec[6]).astype(BF16)
    u = matmul(n2, w_up) + vec[7:11].reshape(hidden)
    cdf, bell = normal_parts(u)
    act = (u * cdf).astype(BF16)
    slope = cdf + u * bell
    layer_out = (x2 + contract_cols(act, w_down) + vec[11]).astype(BF16)

    dy_low = cotangent.reshape(own, width)
    dy = dy_low.astype(F32)
    g_down = contract_rows(dy_low, act).astype(BF16)
    gb_down = jnp.sum(dy, axis=0)
    du = (slope * matmul(dy_low, w_down)).astype(BF16)
    gb_up = jnp.sum(du.astype(F32), axis=0)
    g_up = contract_rows(n2, du).astype(BF16)
    ffn_shard = scatter_rows(jnp.concatenate([g_up, g_down], 1))
    dn2 = contract_cols(du, w_up)
    dx2 = dy + norm_back(dn2, hat_two, factor_two, vec[5])
    g_gain_two = jnp.sum(dn2 * hat_two, axis=0)
    g_shift_two = jnp.sum(dn2, axis=0)
    da = dx2.astype(BF16)
    gb_out = jnp.sum(da.astype(F32), axis=0)
    dctx = contract_cols(da, w_out).astype(BF16)
    g_out = contract_rows(ctx, da).astype(BF16)

    dq, dk, dv, dh = attention_backward(table, qkv, halo_kv, seg_row, seg_keys, dctx, ctx, lse)
    dh = lax.ppermute(dh, "genes", SWAP)
    put = jnp.where(core == 0, own - halo, 0)

    def add_halo(mine, other):
        spread = lax.dynamic_update_slice(jnp.zeros_like(mine), other, (put, 0))
        return (mine.astype(F32) + spread.astype(F32)).astype(BF16)

    dk = add_halo(dk, dh[0])
    dv = add_halo(dv, dh[1])
    dqkv = jnp.concatenate([dq, dk, dv], 1)
    g_qkv = contract_rows(n1, dqkv).astype(BF16)
    dn1 = contract_cols(dqkv, w_qkv)
    gb_query = jnp.sum(dq.astype(F32), axis=0)
    gb_value = jnp.sum(dv.astype(F32), axis=0)
    g_gain_one = jnp.sum(dn1 * hat_one, axis=0)
    g_shift_one = jnp.sum(dn1, axis=0)
    tokens_grad = (dx2 + norm_back(dn1, hat_one, factor_one, vec[0])).reshape(row_count, own, width)
    g_vec = jnp.concatenate(
        [
            jnp.stack(
                [g_gain_one, g_shift_one, gb_query, gb_value, gb_out, g_gain_two, g_shift_two]
            ),
            gb_up.reshape(hidden // width, width),
            gb_down[None],
        ],
        0,
    )
    g_vec = jnp.pad(g_vec.T.astype(BF16), ((0, 0), (0, VEC_COLS - vec_rows)))
    attn_shard = scatter_rows(jnp.concatenate([g_qkv, g_out, g_vec], 1))
    mat_shard = jnp.stack([attn_shard[:, : 4 * width], ffn_shard[:, :hidden], ffn_shard[:, hidden:]])
    vec_shard = attn_shard[:, 4 * width : 4 * width + vec_rows].T
    matrices_out = adamw(matrices, mat_shard, mat_first, mat_second, MATRIX_RATE, MATRIX_DECAY)
    vectors_out = adamw(vectors, vec_shard, vec_first, vec_second, VECTOR_RATE, 0.0)
    return (layer_out.reshape(row_count, own, width), tokens_grad) + matrices_out + vectors_out


def solution(mesh):
    tokens_spec = P("rows", "genes", None)
    mat_spec = P(None, ("rows", "genes"), None)
    vec_spec = P(None, ("rows", "genes"))
    in_specs = (
        tokens_spec,
        P("rows", None),
        tokens_spec,
        mat_spec,
        vec_spec,
        mat_spec,
        mat_spec,
        vec_spec,
        vec_spec,
    )
    out_specs = (tokens_spec,) * 2 + (mat_spec,) * 3 + (vec_spec,) * 3
    return jax.shard_map(
        on_device, mesh=mesh, in_specs=in_specs, out_specs=out_specs, check_vma=False
    )
```

time: 1320 us -> 576 us (0.44)
  matrix products: 650 us -> 98.4 us
  other arithmetic: 165 us -> 45 us
  blocking collectives: 118 us -> 0 us
  Pallas kernels: 0 us -> 98.9 us
  local copies, waits for them, and re-layouts: 142 us -> 43.4 us
  waiting for transfers between devices: 220 us -> 267 us
    dot_general x32 -> x4, matrix products: 584 us -> 44.1 us  [matmul(): lax.dot_general(former, latter, (((1,), (0,)), ((), ())), preferred_eleme...]
    unnamed x2 -> x6, waiting for transfers between devices: 0.03 us -> 196 us
    reduce_scatter x1 -> x0, waiting for transfers between devices: 164 us -> none  [on_device(): lax.psum_scatter(jnp.stack([grad_attention, grad_up, grad_down]), ('rows'...]
    pallas_call x0 -> x2, Pallas kernels: none -> 98.9 us  [the longest x1 49.7 us: attention_backward(): pl.pallas_call(attn_backward_kernel, grid_spec=pltpu.PrefetchScalarGridSp...]
    reduce_sum x14 -> x11, other arithmetic: 62.4 us -> 15.7 us  [the longest x1 3.98 us: on_device(): g_gain_two = jnp.sum(dn2 * hat_two, axis=0)]
    unnamed x6 -> x1, other arithmetic: 46.2 us -> 0.01 us
    all_gather x1 -> x0, blocking collectives: 44.6 us -> none  [on_device(): lax.all_gather(vectors.astype(jnp.bfloat16), ('rows', 'genes'), axis=1, t...]
    unnamed x1 -> x0, blocking collectives: 43.1 us -> none
  transfers between devices with their start and end apart: 2 -> 6, of which waited for: 2 -> 4; matrix products, arithmetic and copies ran while one was open for 4% -> 14% of each run, Pallas kernels for 0% -> 9%
where the time goes in v1:
time: 576 us; the launch traced here: 568 us
  waiting for transfers between devices  267 us (46%)
  Pallas kernels  98.9 us (17%)
  matrix products  98.4 us (17%)
  other arithmetic  45 us (8%)
  local copies, waits for them, and re-layouts  43.4 us (8%)
  between operations  14.7 us (3%)
    unnamed x6, waiting for transfers between devices  196 us
    all_gather x2, waiting for transfers between devices, gather_rows(): return lax.all_gather(shard, BOTH, axis=0, tiled=True)  71.4 us
    pallas_call x1, Pallas kernels, attention_backward(): pl.pallas_call(attn_backward_kernel, grid_spec=pltpu.PrefetchScalarGridSp...  49.7 us
    pallas_call x1, Pallas kernels, attention_forward(): pl.pallas_call(attn_forward_kernel, grid_spec=pltpu.PrefetchScalarGridSpe...  49.1 us
    dot_general x4, matrix products, matmul(): lax.dot_general(former, latter, (((1,), (0,)), ((), ())), preferred_eleme...  44.1 us
    dot_general x4, matrix products, contract_rows(): lax.dot_general(former, latter, (((0,), (0,)), ((), ())), preferred_eleme...  27.8 us
    dot_general x4, matrix products, contract_cols(): lax.dot_general(former, latter, (((1,), (1,)), ((), ())), preferred_eleme...  26.5 us
    unnamed x80, local copies, waits for them, and re-layouts  16.8 us
  transfers between devices with their start and end apart: 6, of which 4 were waited for; matrix products, arithmetic and copies ran while one was open for 14% of the time, Pallas kernels for 9%

profile of v1, /device:TPU:0, one launch (start us, length us, event | category | flops | bytes accessed | tf_op | source)
XLA Modules:
  0.0 568.3 jit_solution(4253132327614993038)
XLA Ops:
  7.2 1.3 convert_element_type.122
  12.5 62.3 %all-gather.3.cloned.1.call-done = bf16[768,2432]{1,0:T(8,128)(2,1)} async-done(((bf16[24,2432]{1,0:T(8,128)(2,1)}), bf16[768,2432]{1,0:T(8,128)(2,1)}) %all-gather.3.cloned.1.call-update) | async-done | bytes 3735568 | tf_op jit(solution)/shard_map/all_gather | solution.py:310
  74.9 1.1 convert_bitcast_fusion.1
  76.0 1.8 slice_reduce_fusion.2
  77.8 4.4 add_convert_fusion.q_ref.k_ref.v_ref
  82.2 2.1 copy-done.2
  84.4 1.3 constant_dynamic-slice_fusion.2
  87.6 1.4 convert_reduce_fusion.4
  92.1 1.3 copy.222
  93.4 1.2 add_bitcast_fusion
  94.7 1.3 copy.218
  96.0 2.6 copy.229
  102.3 1.1 copy.227
  104.1 1.4 broadcast_in_dim.8.segk_ref
  105.5 49.1 %attn_forward.1 = (bf16[1024,768]{1,0:T(8,128)(2,1)}, f32[6,2,1024]{2,1,0:T(2,128)}) custom-call(s32[4,7]{1,0:T(4,128)} %pad_add_fusion.1.table, bf16[1024,2304]{1,0:T(8,128)(2,1)} %copy-done.2, bf16[1024,2304]{1,0:T(8,128)(2,1)} %copy-done.2, bf16[1024,2304]{1,0:T(8,128)(2,1)} %copy-done.2, bf16[512,1536]{1,0:T(8,128)(2,1)} %copy-done.6, ...), custom_call_target="tpu_custom_call" | custom-call | tf_op jit(solution)/shard_map/attn_forward/pallas_call | solution.py:248
  154.6 9.1 %all-gather.5.cloned.1.call-done = bf16[768,6912]{1,0:T(8,128)(2,1)} async-done(((bf16[24,6912]{1,0:T(8,128)(2,1)}), bf16[768,6912]{1,0:T(8,128)(2,1)}) %all-gather.5.cloned.1.call-update) | async-done | bytes 10616848 | tf_op jit(solution)/shard_map/all_gather | solution.py:310
  163.6 3.5 fusion.70
  167.9 1.5 slice-done.2
  169.4 18.9 %multiply_convert_fusion = (bf16[1024,3072]{1,0:T(8,128)(2,1)}, f32[1024,3072]{1,0:T(8,128)}) fusion(f32[3072]{0:T(1024)S(1)} %copy-done.21, bf16[768,6912]{1,0:T(8,128)(2,1)S(1)} %bitcast.121, f32[1024,768]{0,1:T(8,128)S(1)} %get-tuple-element.104, f32[768]{0:T(1024)S(1)} %copy-done.29, f32[768]{0:T(1024)S(1)} %copy-done.18, f32[1024]{0:T(1024)S(1)} %add_rsqrt_fusion, ...), kind=kOutput, calls=%fused_computation.5 | convolution fusion | flops 4908122112 | bytes 26767360 | tf_op jit(solution)/shard_map/dot_general | solution.py:42
  188.4 17.2 %fusion.73 = (bf16[3072]{0:T(1024)(128)(2,1)S(1)}, bf16[1024,3072]{1,0:T(8,128)(2,1)S(1)}) fusion(bf16[768,6912]{1,0:T(8,128)(2,1)S(1)} %bitcast.121, bf16[1,1024,768]{2,1,0:T(8,128)(2,1)S(1)} %copy-done.8, f32[1024,3072]{1,0:T(8,128)} %get-tuple-element.106, f32[3072]{0:T(1024)S(1)} %copy-done.21), kind=kOutput, calls=%fused_computation.179 | convolution fusion | flops 4916769792 | bytes 25184256 | tf_op jit(solution)/shard_map/dot_general | solution.py:42
  205.6 6.8 %fusion.72 = (bf16[768]{0:T(1024)(128)(2,1)S(1)}, f32[1024,768]{1,0:T(8,128)}) fusion(bf16[1024,3072]{1,0:T(8,128)(2,1)S(1)} %get-tuple-element.112, bf16[768,6912]{1,0:T(8,128)(2,1)S(1)} %bitcast.121), kind=kOutput, calls=%fused_computation.178 | convolution fusion | flops 4832623616 | bytes 14157312 | tf_op jit(solution)/shard_map/dot_general | solution.py:36
  212.4 3.5 copy.230
  215.9 4.0 multiply_reduce_fusion
  220.6 2.7 convert_reduce_fusion.5
  223.3 4.8 convolution_convert_fusion.3.grad_ref
  228.1 49.7 %attn_backward.1 = (bf16[1024,768]{1,0:T(8,128)(2,1)}, bf16[1024,768]{1,0:T(8,128)(2,1)}, bf16[1024,768]{1,0:T(8,128)(2,1)}, bf16[2,512,768]{2,1,0:T(8,128)(2,1)}) custom-call(s32[4,7]{1,0:T(4,128)} %pad_add_fusion.1.table, bf16[1024,2304]{1,0:T(8,128)(2,1)} %copy-done.2, bf16[1024,2304]{1,0:T(8,128)(2,1)} %copy-done.2, bf16[1024,2304]{1,0:T(8,128)(2,1)} %copy-done.2, ...), custom_call_target="tpu_custom_call" | custom-call | tf_op jit(solution)/shard_map/attn_backward/pallas_call | solution.py:274
  278.3 1.7 reduce.1
  280.0 4.8 convolution_convert_fusion.4
  285.0 1.3 fusion.44
  287.0 1.3 fusion.43
  288.9 5.9 %convolution_convert_fusion.2 = bf16[768,2304]{1,0:T(8,128)(2,1)} fusion(bf16[1024,768]{1,0:T(8,128)(2,1)S(1)} %get-tuple-element.95, bf16[1024,768]{1,0:T(8,128)(2,1)S(1)} %add_convert_fusion.2, bf16[1024,768]{1,0:T(8,128)(2,1)S(1)} %copy-done.10, bf16[1,1024,768]{1,2,0:T(8,128)(2,1)S(1)} %copy.209, f32[768]{0:T(1024)S(1)} %copy-done.31, ...), kind=kOutput, calls=%fused_computation.16 | convolution fusion | flops 3644522496 | bytes 9844736 | tf_op jit(solution)/shard_map/dot_general | solution.py:30
  294.9 5.5 fusion.71
  300.4 3.6 copy.231
  304.0 3.0 fusion.27
  307.4 5.5 fusion.3
  312.9 8.6 %convolution_convert_fusion.1 = bf16[768,3072]{1,0:T(8,128)(2,1)S(1)} fusion(bf16[1024,3072]{1,0:T(8,128)(2,1)} %copy-done.33, f32[1024,768]{0,1:T(8,128)} %copy-done.3, f32[768]{0:T(1024)S(1)} %copy-done.29, f32[768]{0:T(1024)S(1)} %copy-done.18, f32[1024]{0:T(1024)S(1)} %add_rsqrt_fusion, f32[1024]{0:T(1024)S(1)} %broadcast_multiply_fusion.4), kind=kOutput, calls=%fused_computation.15 | convolution fusion | flops 4838129664 | bytes 14170112 | tf_op jit(solution)/shard_map/dot_general | solution.py:30
  321.5 8.4 %fusion.4 = bf16[768,3072]{1,0:T(8,128)(2,1)S(1)} fusion(bf16[1024,3072]{1,0:T(8,128)(2,1)} %get-tuple-element.105, bf16[1,1024,768]{2,1,0:T(8,128)(2,1)S(1)} %copy-done.8), kind=kOutput, calls=%fused_computation.19 | convolution fusion | flops 4834197504 | bytes 12582912 | tf_op jit(solution)/shard_map/dot_general | solution.py:30
  330.0 4.0 pad_maximum_fusion
  334.7 9.4 %fusion.37 = bf16[1,1024,768]{1,2,0:T(8,128)(2,1)S(1)} fusion(f32[768]{0:T(1024)S(1)} %copy-done.28, f32[1024,768]{0,1:T(8,128)} %copy-done.3, bf16[1024,3072]{1,0:T(8,128)(2,1)} %get-tuple-element.105, bf16[768,6912]{1,0:T(8,128)(2,1)} %all-gather.5.cloned.1.call-done), kind=kOutput, calls=%fused_computation.68 | convolution fusion | flops 4834197504 | bytes 15731712 | tf_op jit(solution)/shard_map/dot_general | solution.py:36
  344.1 1.6 copy.242
  345.6 5.5 fusion.26
  351.2 3.9 copy.243
  355.0 57.7 %reduce-scatter.9.cloned.1.call-done = bf16[24,3200]{1,0:T(8,128)(2,1)} async-done(((bf16[768,3200]{1,0:T(8,128)(2,1)}), bf16[24,3200]{1,0:T(8,128)(2,1)}) %reduce-scatter.9.cloned.1.call-update) | async-done | bytes 153616
  412.8 1.4 copy.236
  415.5 138.3 %reduce-scatter.7.cloned.1.call-done = bf16[24,6144]{1,0:T(8,128)(2,1)} async-done(((bf16[768,6144]{1,0:T(8,128)(2,1)}), bf16[24,6144]{1,0:T(8,128)(2,1)}) %reduce-scatter.7.cloned.1.call-update) | async-done | bytes 294928
  553.8 1.7 copy.248
  555.9 1.2 copy.240
  557.5 3.8 multiply_subtract_fusion
  (143 shorter events, 19.9 us)
Async XLA Ops:
  7.2 78.7 %copy-start = (s32[1,2048]{1,0:T(1,128)S(1)}, s32[1,2048]{1,0:T(1,128)}, u32[]{:S(2)}) copy-start(s32[1,2048]{1,0:T(1,128)} %param.10) | copy-start | bytes 24580
  7.2 3.8 copy-start.9
  7.2 67.7 %all-gather.3.cloned.1.call-start = ((), (), s32[]{:S(2)}) async-start(), calls=%async_computation.2 | async-start | bytes 3852288 | tf_op jit(solution)/shard_map/all_gather | solution.py:310
  10.1 153.6 %all-gather.5.cloned.1.call-start = ((), (), s32[]{:S(2)}) async-start(), calls=%async_computation.3 | async-start | bytes 10948608 | tf_op jit(solution)/shard_map/all_gather | solution.py:310
  10.9 401.8 %reduce-scatter.9.cloned.1.call-start = ((), (), s32[]{:S(2)}) async-start(), calls=%async_computation.5 | async-start | bytes 5068800
  12.5 69.7 %copy-start.16 = (f32[1024]{0:T(1024)}, f32[1024]{0:T(1024)S(1)}, u32[]{:S(2)}) copy-start(f32[1024]{0:T(1024)S(1)} %add_rsqrt_fusion.1) | copy-start | bytes 12292
  74.8 2.9 copy-start.22
  77.8 4.5 copy-start.14
  77.8 4.5 copy-start.30
  82.2 2.1 copy-start.2
  85.6 18.4 %collective-permute-start = (bf16[512,1536]{1,0:T(8,128)(2,1)}, bf16[512,1536]{1,0:T(8,128)(2,1)S(1)}, u32[]{:S(2)}, u32[]{:S(2)}) collective-permute-start(bf16[512,1536]{1,0:T(8,128)(2,1)} %constant_dynamic-slice_fusion.2), channel_id=1, source_target_pairs={{0,1},{1,0},{2,3},{3,2},{4,5},{5,4},{6,7},{7,6},{8,9},{9,8},{10,11... | collective-permute-start | bytes 4718600 | tf_op jit(solution)/shard_map/ppermute | solution.py:351
  85.9 19.5 %copy-start.13 = (s32[1,1024]{1,0:T(1,128)}, s32[1,1024]{1,0:T(1,128)S(1)}, u32[]{:S(2)}) copy-start(s32[1,1024]{1,0:T(1,128)S(1)} %constant_dynamic-slice_fusion.1.segq_ref) | copy-start | bytes 12292
  87.1 0.6 copy-start.20
  89.1 1.5 copy-start.27
  90.0 1.4 copy-start.26
  104.0 1.4 copy-start.6
  105.5 58.2 %copy-start.32 = (f32[768]{0:T(1024)S(1)}, f32[768]{0:T(1024)}, u32[]{:S(2)}) copy-start(f32[768]{0:T(1024)} %get-tuple-element.77) | copy-start | bytes 9220
  163.6 4.0 slice-start
  163.6 4.3 slice-start.1
  163.6 5.8 %slice-start.2 = ((s8[10616832]{0:T(1024)(128)(4,1)}), s8[2228224]{0:T(1024)(128)(4,1)S(1)}, s32[]{:S(2)}) async-start(s8[10616832]{0:T(1024)(128)(4,1)} %bitcast.120), calls=%async_computation.8 | async-start | bytes 4456448
  167.2 21.2 %copy-start.3 = (f32[1024,768]{0,1:T(8,128)}, f32[1024,768]{0,1:T(8,128)S(1)}, u32[]{:S(2)}) copy-start(f32[1024,768]{0,1:T(8,128)S(1)} %get-tuple-element.104) | copy-start | bytes 9437188
  167.2 2.2 copy-start.18
  167.2 2.2 copy-start.21
  167.2 2.2 copy-start.29
  169.4 18.9 %copy-start.8 = (bf16[1,1024,768]{2,1,0:T(8,128)(2,1)S(1)}, bf16[1,1024,768]{2,1,0:T(8,128)(2,1)}, u32[]{:S(2)}) copy-start(bf16[1,1024,768]{2,1,0:T(8,128)(2,1)} %param.11) | copy-start | bytes 4718596
  205.6 6.8 %copy-start.33 = (bf16[1024,3072]{1,0:T(8,128)(2,1)}, bf16[1024,3072]{1,0:T(8,128)(2,1)S(1)}, u32[]{:S(2)}) copy-start(bf16[1024,3072]{1,0:T(8,128)(2,1)S(1)} %get-tuple-element.112) | copy-start | bytes 18874372
  215.9 4.0 copy-start.4
  215.9 4.7 copy-start.5
  223.3 4.8 copy-start.7
  277.9 7.0 %collective-permute-start.1 = (bf16[2,512,768]{2,1,0:T(8,128)(2,1)}, bf16[2,512,768]{2,1,0:T(8,128)(2,1)}, u32[]{:S(2)}, u32[]{:S(2)}) collective-permute-start(bf16[2,512,768]{2,1,0:T(8,128)(2,1)} %get-tuple-element.18), channel_id=1, source_target_pairs={{0,1},{1,0},{2,3},{3,2},{4,5},{5,4},{6,7},{7,6},{8,9},{9,8},{10,11... | collective-permute-start | bytes 4718600 | tf_op jit(solution)/shard_map/ppermute | solution.py:383
  284.8 1.6 copy-start.12
  286.5 1.9 copy-start.11
  287.0 1.9 copy-start.10
  287.0 1.9 copy-start.15
  287.0 1.9 copy-start.17
  287.0 1.9 copy-start.31
  288.9 6.0 %copy-start.23 = (bf16[768,2432]{1,0:T(8,128)(2,1)S(1)}, bf16[768,2432]{1,0:T(8,128)(2,1)}, u32[]{:S(2)}) copy-start(bf16[768,2432]{1,0:T(8,128)(2,1)} %all-gather.3.cloned.1.call-done) | copy-start | bytes 11206660
  312.9 240.9 %reduce-scatter.7.cloned.1.call-start = ((), (), s32[]{:S(2)}) async-start(), calls=%async_computation.4 | async-start | bytes 9732096
  334.0 0.7 copy-start.28
  414.2 0.7 copy-start.19
  414.2 0.7 copy-start.24
  414.2 0.7 copy-start.25
  557.1 4.2 copy-start.1
Sparse Core Ops, SparseCore 0:
  11.5 63.3 all-gather.2
  78.3 85.2 all-gather.4
  313.0 99.7 reduce-scatter.8
  418.5 135.2 reduce-scatter.6
